TPU v7x, 32 devices: a whole 2x2x4 slice. The times are simulated.
32 devices in a mesh: req: 8 (over z, y), mdl: 4 (over x, core).
Axes of the slice: x: 2, y: 2, z: 4, core: 2. Of those that a mesh axis runs over, the one named last changes fastest.
Arguments:
- tokens: bfloat16 [2048, 1024], P('req', 'mdl'), may hold values from -6 to 6
- perm: int32 [32], replicated, may hold values from 0 to 31, each once
- w_query: bfloat16 [1024, 1024], P(None, 'mdl'), may hold values from -0.1875 to 0.1875
- q_bias: bfloat16 [1024], P('mdl'), may hold values from -6 to 6
- w_key: bfloat16 [1024, 1024], P(None, 'mdl'), may hold values from -0.1875 to 0.1875
- w_value: bfloat16 [1024, 1024], P(None, 'mdl'), may hold values from -0.1875 to 0.1875
- w_out: bfloat16 [1024, 1024], P('mdl'), may hold values from -0.1875 to 0.1875
- norm_gain: float32 [1024], P('mdl'), may hold values from 0.5 to 1.5
- norm_bias: float32 [1024], P('mdl'), may hold values from -3 to 3
- w_fc1: bfloat16 [1024, 2048], P(None, 'mdl'), may hold values from -0.1875 to 0.1875
- fc1_bias: float32 [2048], P('mdl'), may hold values from -4 to 4
- w_fc2: bfloat16 [2048, 1024], P('mdl'), may hold values from -0.125 to 0.125
- fc2_bias: float32 [1024], P('mdl'), may hold values from -3 to 3
- final_gain: float32 [1024], P('mdl'), may hold values from 0.5 to 1.5
- final_bias: float32 [1024], P('mdl'), may hold values from -3 to 3
- key_pool: bfloat16 [56, 128, 1024], P('req', None, 'mdl'), may hold values from -1000 to 1000
- value_pool: bfloat16 [56, 128, 1024], P('req', None, 'mdl'), may hold values from -6 to 6
- page_table: int32 [32, 4], P('req'), may hold values from 0 to 55, as said below
- cache_len: int32 [32], P('req'), may hold values from 1 to 512, as said below
- parents: int32 [32, 64], P('req'), may hold values from -1 to 62, as said below
- accepted: int32 [32, 8], P('req'), may hold values from 0 to 63
Outputs:
- layer_out: bfloat16 [2048, 1024], P('req', 'mdl')
- kept_keys: bfloat16 [32, 8, 1024], P('req', None, 'mdl')
- kept_values: bfloat16 [32, 8, 1024], P('req', None, 'mdl')
Inputs may be any that keep to these rules, and one draw needn't show every extreme that they name: `page_table`: every entry of row s names a page held by index s // 4 of req, that is one of pages (s // 4) * 7 to (s // 4) * 7 + 6; the pages that the slots of one index of req use are distinct. `cache_len`: the lengths of the slots of one index of req use at most 7 pages together. parents[s, 0] = -1 and 0 <= parents[s, i] < i for i > 0.
All inputs are finite; a program needn't handle non-finite values.
Results may differ from a plain program's by a relative error of at most 0.01.
Values may be sent and summed in bfloat16 or wider, within the bound.
A program may use at most 64 MiB of HBM per device.

v0:
```python
import jax
import jax.numpy as jnp
from jax import lax
from jax.sharding import PartitionSpec as P

HD = 64


def ancestry(parents):
    draft_len = parents.shape[-1]
    node_ids = jnp.arange(draft_len, dtype=jnp.int32)
    hop_matrix = (parents[..., :, None] == node_ids).astype(jnp.bfloat16)
    reached = jnp.broadcast_to(jnp.eye(draft_len, dtype=jnp.bfloat16), hop_matrix.shape)
    for doubling in range((draft_len - 1).bit_length()):
        grown = jnp.einsum("rij,rjk->rik", reached, hop_matrix, preferred_element_type=jnp.float32)
        squared = jnp.einsum(
            "rij,rjk->rik", hop_matrix, hop_matrix, preferred_element_type=jnp.float32
        )
        reached = jnp.minimum(reached.astype(jnp.float32) + grown, 1.0).astype(jnp.bfloat16)
        hop_matrix = jnp.minimum(squared, 1.0).astype(jnp.bfloat16)
    return reached > 0.5


def outgoing_rows(perm, rows_dev, req_count, my_index):
    requests = perm.shape[0]
    per_dev = requests // req_count
    block_count = max(1, rows_dev // requests)
    target = jnp.arange(req_count, dtype=jnp.int32)[:, None, None]
    lane_index = jnp.arange(per_dev, dtype=jnp.int32)[None, :, None]
    offset = jnp.arange(block_count, dtype=jnp.int32)[None, None, :]
    request = perm[target * per_dev + lane_index]
    first_pos = my_index * rows_dev // requests
    local_row = (first_pos + offset) * requests + request - my_index * rows_dev
    usable = (local_row >= 0) & (local_row < rows_dev)
    return (jnp.clip(local_row, 0, rows_dev - 1).reshape(-1), usable.reshape(-1))


def incoming_rows(perm, rows_dev, req_count, my_index, draft_len):
    requests = perm.shape[0]
    per_dev = requests // req_count
    block_count = max(1, rows_dev // requests)
    slot_count = per_dev * block_count
    lane_index = jnp.arange(per_dev, dtype=jnp.int32)[:, None]
    position = jnp.arange(draft_len, dtype=jnp.int32)[None, :]
    request = perm[my_index * per_dev + lane_index]
    flat_pos = position * requests + request
    source = flat_pos // rows_dev
    offset = flat_pos % rows_dev // requests
    return (source * slot_count + lane_index * block_count + offset).reshape(-1)


def returning_rows(perm, rows_dev, req_count, my_index, draft_len):
    requests = perm.shape[0]
    per_dev = requests // req_count
    block_count = max(1, rows_dev // requests)
    source = jnp.arange(req_count, dtype=jnp.int32)[:, None, None]
    lane_index = jnp.arange(per_dev, dtype=jnp.int32)[None, :, None]
    offset = jnp.arange(block_count, dtype=jnp.int32)[None, None, :]
    request = perm[my_index * per_dev + lane_index]
    position = source * rows_dev // requests + offset
    usable = ((position * requests + request) // rows_dev == source) & (position < draft_len)
    row_index = lane_index * draft_len + jnp.clip(position, 0, draft_len - 1)
    return (row_index.reshape(-1), usable.reshape(-1))


def arriving_rows(perm, rows_dev, req_count, my_index):
    requests = perm.shape[0]
    per_dev = requests // req_count
    block_count = max(1, rows_dev // requests)
    slot_count = per_dev * block_count
    inverse = jnp.zeros((requests,), jnp.int32).at[perm].set(jnp.arange(requests, dtype=jnp.int32))
    local_row = jnp.arange(rows_dev, dtype=jnp.int32)
    request = (my_index * rows_dev + local_row) % requests
    slot_of = inverse[request]
    offset = local_row // requests
    return slot_of // per_dev * slot_count + slot_of % per_dev * block_count + offset


def attend(query, keys_new, values_new, key_pool, value_pool, local_pages, cache_len, parents):
    per_dev, draft_len, part_width = query.shape
    head_count = part_width // HD
    cache_keys = jnp.transpose(
        key_pool[local_pages].reshape(per_dev, -1, head_count, HD), (0, 2, 1, 3)
    )
    cache_values = jnp.transpose(
        value_pool[local_pages].reshape(per_dev, -1, head_count, HD), (0, 2, 1, 3)
    )
    key_span = cache_keys.shape[2]
    query_heads = jnp.transpose(query.reshape(per_dev, draft_len, head_count, HD), (0, 2, 1, 3))
    draft_keys = jnp.transpose(keys_new.reshape(per_dev, draft_len, head_count, HD), (0, 2, 1, 3))
    draft_values = jnp.transpose(
        values_new.reshape(per_dev, draft_len, head_count, HD), (0, 2, 1, 3)
    )
    score_scale = HD ** (-0.5)
    cache_scores = (
        jnp.einsum("rhqe,rhke->rhqk", query_heads, cache_keys, preferred_element_type=jnp.float32)
        * score_scale
    )
    draft_scores = (
        jnp.einsum("rhqe,rhke->rhqk", query_heads, draft_keys, preferred_element_type=jnp.float32)
        * score_scale
    )
    in_range = jnp.arange(key_span, dtype=jnp.int32)[None, :] < cache_len[:, None]
    tree_mask = ancestry(parents)
    cache_scores = jnp.where(in_range[:, None, None, :], cache_scores, -1e30)
    draft_scores = jnp.where(tree_mask[:, None, :, :], draft_scores, -1e30)
    highest = jnp.maximum(cache_scores.max(-1), draft_scores.max(-1))[..., None]
    cache_weight = jnp.exp(cache_scores - highest)
    draft_weight = jnp.exp(draft_scores - highest)
    weight_sum = cache_weight.sum(-1, keepdims=True) + draft_weight.sum(-1, keepdims=True)
    cache_probs = (cache_weight / weight_sum).astype(jnp.bfloat16)
    draft_probs = (draft_weight / weight_sum).astype(jnp.bfloat16)
    mixed = jnp.einsum(
        "rhqk,rhke->rhqe", cache_probs, cache_values, preferred_element_type=jnp.float32
    )
    mixed = mixed + jnp.einsum(
        "rhqk,rhke->rhqe", draft_probs, draft_values, preferred_element_type=jnp.float32
    )
    mixed = jnp.transpose(mixed, (0, 2, 1, 3))
    return mixed.reshape(per_dev, draft_len, part_width).astype(jnp.bfloat16)


def fold_features(row_part, weights):
    piece = lax.all_gather(row_part, "mdl", axis=1, tiled=True)
    return tuple((jnp.dot(piece, weight, preferred_element_type=jnp.float32) for weight in weights))


def reduce_groups(partial_value):
    return lax.psum_scatter(
        partial_value.astype(jnp.bfloat16), "mdl", scatter_dimension=1, tiled=True
    ).astype(jnp.float32)


def normalize(hidden, gain, bias):
    full_width = hidden.shape[1] * lax.axis_size("mdl")
    sum_first, sum_second = lax.psum(
        (jnp.sum(hidden, axis=1), jnp.sum(hidden * hidden, axis=1)), "mdl"
    )
    row_mean = sum_first / full_width
    row_var = sum_second / full_width - row_mean * row_mean
    return (
        (hidden - row_mean[:, None]) * lax.rsqrt(row_var + 1e-05)[:, None] * gain + bias
    ).astype(jnp.bfloat16)


def per_device(
    tokens,
    perm,
    w_query,
    q_bias,
    w_key,
    w_value,
    w_out,
    norm_gain,
    norm_bias,
    w_fc1,
    fc1_bias,
    w_fc2,
    fc2_bias,
    final_gain,
    final_bias,
    key_pool,
    value_pool,
    page_table,
    cache_len,
    parents,
    accepted,
):
    req_count = lax.axis_size("req")
    my_index = lax.axis_index("req")
    rows_dev, part_width = tokens.shape
    per_dev, draft_len = parents.shape
    pages_dev = key_pool.shape[0]
    send_rows, send_usable = outgoing_rows(perm, rows_dev, req_count, my_index)
    take_rows = incoming_rows(perm, rows_dev, req_count, my_index, draft_len)
    back_rows, back_usable = returning_rows(perm, rows_dev, req_count, my_index, draft_len)
    home_rows = arriving_rows(perm, rows_dev, req_count, my_index)
    slot_count = send_rows.shape[0] // req_count
    local_pages = page_table - my_index * pages_dev
    query_sum, key_sum, value_sum = fold_features(tokens, (w_query, w_key, w_value))
    query = (query_sum + q_bias.astype(jnp.float32)).astype(jnp.bfloat16)
    query, keys_new, values_new = (
        query,
        key_sum.astype(jnp.bfloat16),
        value_sum.astype(jnp.bfloat16),
    )
    packed = jnp.concatenate([query, keys_new, values_new], axis=1)
    outgoing = jnp.where(send_usable[:, None], packed[send_rows], 0).reshape(
        req_count, slot_count, 3 * part_width
    )
    arrived = lax.all_to_all(outgoing, "req", split_axis=0, concat_axis=0, tiled=True)
    served = arrived.reshape(req_count * slot_count, 3 * part_width)[take_rows].reshape(
        per_dev, draft_len, 3 * part_width
    )
    served_query = served[:, :, :part_width]
    served_keys = served[:, :, part_width : 2 * part_width]
    served_values = served[:, :, 2 * part_width :]
    attended = attend(
        served_query,
        served_keys,
        served_values,
        key_pool,
        value_pool,
        local_pages,
        cache_len,
        parents,
    )
    flat_rows = attended.reshape(per_dev * draft_len, part_width)
    back = jnp.where(back_usable[:, None], flat_rows[back_rows], 0).reshape(
        req_count, slot_count, part_width
    )
    returned = lax.all_to_all(back, "req", split_axis=0, concat_axis=0, tiled=True)
    home = returned.reshape(req_count * slot_count, part_width)[home_rows]
    summed = reduce_groups(jnp.dot(home, w_out, preferred_element_type=jnp.float32))
    normed_first = normalize(tokens.astype(jnp.float32) + summed, norm_gain, norm_bias)
    inner = fold_features(normed_first, (w_fc1,))[0]
    activated = jax.nn.gelu(inner + fc1_bias, approximate=False).astype(jnp.bfloat16)
    ff_summed = reduce_groups(jnp.dot(activated, w_fc2, preferred_element_type=jnp.float32))
    second_hidden = normed_first.astype(jnp.float32) + ff_summed + fc2_bias
    layer_out = normalize(second_hidden, final_gain, final_bias)
    kept_keys = jnp.take_along_axis(served_keys, accepted[:, :, None], axis=1)
    kept_values = jnp.take_along_axis(served_values, accepted[:, :, None], axis=1)
    return (layer_out, kept_keys, kept_values)


def solution(mesh):
    in_specs = (
        P("req", "mdl"),
        P(),
        P(None, "mdl"),
        P("mdl"),
        P(None, "mdl"),
        P(None, "mdl"),
        P("mdl", None),
        P("mdl"),
        P("mdl"),
        P(None, "mdl"),
        P("mdl"),
        P("mdl", None),
        P("mdl"),
        P("mdl"),
        P("mdl"),
        P("req", None, "mdl"),
        P("req", None, "mdl"),
        P("req", None),
        P("req"),
        P("req", None),
        P("req", None),
    )
    out_specs = (P("req", "mdl"), P("req", None, "mdl"), P("req", None, "mdl"))
    return jax.shard_map(
        per_device, mesh=mesh, in_specs=in_specs, out_specs=out_specs, check_vma=False
    )
```

profile of v0, /device:TPU:0, one launch (start us, length us, event | category | flops | bytes accessed | tf_op | source)
XLA Modules:
  0.0 171.7 jit_solution(14824741768853635884)
XLA Ops:
  8.9 8.6 %all_gather.6 = bf16[256,1024]{1,0:T(8,128)(2,1)S(1)} all-gather(bf16[256,256]{1,0:T(8,128)(2,1)S(1)} %copy-done.4), channel_id=1, replica_groups=mesh['req'=8,'mdl'=4] {'mdl'}, dimensions={1}, use_global_device_ids=true | all-gather | bytes 655360 | tf_op jit(solution)/shard_map/all_gather | solution.py:124
  19.1 1.2 gather_fusion.2
  21.2 5.8 %all-to-all-start = ((bf16[8,32,768]{2,1,0:T(8,128)(2,1)}), bf16[8,32,768]{2,1,0:T(8,128)(2,1)S(1)}, u32[]{:S(2)}, u32[]{:S(2)}) async-start(bf16[8,32,768]{2,1,0:T(8,128)(2,1)} %broadcast_select_fusion), calls=%async_computation | async-start | bytes 786432 | tf_op jit(solution)/shard_map/all_to_all | solution.py:191
  35.7 1.1 copy.31
  36.8 1.3 reshape.769
  42.5 1.2 reshape.771
  45.2 4.6 %compare_select_fusion.10 = s32[256,1]{0,1:T(1,128)S(1)} fusion(s32[]{:T(128)} %bitcast.41, s32[]{:T(128)} %bitcast.42, s32[]{:T(128)} %bitcast.43, s32[]{:T(128)} %bitcast.44, s32[]{:T(128)} %bitcast.45, s32[]{:T(128)} %bitcast.47, s32[]{:T(128)} %bitcast.46, s32[]{:T(128)S(6)} %mul.188), kind=kLoop, calls=%fused_computation.205 | loop fusion | flops 6912 | bytes 1056 | tf_op jit(solution)/shard_map/gather | solution.py:74
  51.1 16.1 %select_select_fusion = s32[256]{0:T(256)} fusion(pred[256]{0:T(512)(128)(4,1)S(1)} %copy-done.33, pred[256]{0:T(512)(128)(4,1)S(1)} %copy-done.34, pred[256]{0:T(512)(128)(4,1)S(1)} %copy-done.35, pred[256]{0:T(512)(128)(4,1)S(1)} %copy-done.36, pred[256]{0:T(512)(128)(4,1)S(1)} %get-tuple-element.63, pred[256]{0:T(512)(128)(4,1)S(1)} %get-tuple-element.64, ...), kind=kLoop, calls=%fused_computation.246 | loop fusion | flops 6400 | bytes 8548 | tf_op jit(solution)/shard_map/gather | solution.py:74
  67.2 1.3 gather_fusion.4
  70.3 2.0 %fusion = (f32[4,4,64]{2,1,0:T(4,128)S(1)}, f32[4,4,64,512]{3,2,1,0:T(8,128)S(1)}) fusion(pred[4,512]{1,0:T(4,128)(4,1)S(1)} %iota_compare_fusion.4, bf16[4,4,512,64]{2,0,3,1:T(4,128)(2,1)} %bitcast.121, bf16[4,64,4,64]{3,2,1,0:T(4,128)(2,1)} %reshape.768), kind=kOutput, calls=%fused_computation.15 | convolution fusion | flops 68680704 | bytes 3282944 | tf_op jit(solution)/shard_map/rhqe,rhke->rhqk/dot_general | solution.py:96
  73.6 1.9 %fusion.1 = f32[4,4,64]{2,1,0:T(4,128)} fusion(f32[4,4,64,512]{3,2,1,0:T(8,128)S(1)} %get-tuple-element.56, f32[4,4,64]{2,1,0:T(4,128)S(1)} %max.17, pred[4,512]{1,0:T(4,128)(4,1)} %copy-done.20), kind=kLoop, calls=%fused_computation.16 | loop fusion | flops 2096128 | bytes 2107392 | tf_op jit(solution)/shard_map/reduce_sum | solution.py:110
  76.5 1.3 fusion.39
  79.2 1.4 gather_fusion.7
  81.4 6.0 %all-to-all-start.1 = ((bf16[8,32,256]{2,1,0:T(8,128)(2,1)}), bf16[8,32,256]{2,1,0:T(8,128)(2,1)S(1)}, u32[]{:S(2)}, u32[]{:S(2)}) async-start(bf16[8,32,256]{2,1,0:T(8,128)(2,1)} %broadcast_select_fusion.1), calls=%async_computation.1 | async-start | bytes 262144 | tf_op jit(solution)/shard_map/all_to_all | solution.py:212
  87.6 7.1 %all-to-all-done.1 = bf16[8,32,256]{2,1,0:T(8,128)(2,1)S(1)} async-done(((bf16[8,32,256]{2,1,0:T(8,128)(2,1)}), bf16[8,32,256]{2,1,0:T(8,128)(2,1)S(1)}, u32[]{:S(2)}, u32[]{:S(2)}) %all-to-all-start.1) | async-done | bytes 131104 | tf_op jit(solution)/shard_map/all_to_all | solution.py:212
  94.7 1.2 gather_fusion.8
  95.9 1.1 convolution_convert_fusion.1
  97.1 19.1 %reduce-scatter.3.cloned.1.call-done = bf16[256,256]{1,0:T(8,128)(2,1)} async-done(((bf16[256,1024]{1,0:T(8,128)(2,1)}), bf16[256,256]{1,0:T(8,128)(2,1)}) %reduce-scatter.3.cloned.1.call-update) | async-done | bytes 131088 | tf_op jit(solution)/shard_map/reduce_scatter | solution.py:129
  117.3 5.8 %all-reduce.1 = (f32[256]{0:T(256)S(1)}, f32[256]{0:T(256)S(1)}) all-reduce(f32[256]{0:T(256)S(1)} %get-tuple-element.7, f32[256]{0:T(256)S(1)} %get-tuple-element.6), channel_id=1, replica_groups=mesh['req'=8,'mdl'=4] {'mdl'}, use_global_device_ids=true, to_apply=%region_9.10 | all-reduce | flops 512 | bytes 4096 | tf_op jit(solution)/shard_map/psum | solution.py:136
  124.1 7.3 %all_gather.7 = bf16[256,1024]{1,0:T(8,128)(2,1)S(1)} all-gather(bf16[256,256]{1,0:T(8,128)(2,1)S(1)} %add_convert_fusion.1), channel_id=1, replica_groups=mesh['req'=8,'mdl'=4] {'mdl'}, dimensions={1}, use_global_device_ids=true | all-gather | bytes 655360 | tf_op jit(solution)/shard_map/all_gather | solution.py:124
  131.5 2.7 %convolution_convert_fusion = bf16[256,1024]{1,0:T(8,128)(2,1)} fusion(bf16[512,1024]{1,0:T(8,128)(2,1)S(1)} %copy-done, bf16[256,1024]{1,0:T(8,128)(2,1)S(1)} %all_gather.7, bf16[1024,512]{1,0:T(8,128)(2,1)S(1)} %copy-done.41, f32[512]{0:T(512)S(1)} %copy-done.43), kind=kOutput, calls=%fused_computation.17 | convolution fusion | flops 545783808 | bytes 3147776 | tf_op jit(solution)/shard_map/dot_general | solution.py:218
  136.4 19.9 %reduce-scatter.5.cloned.1.call-done = bf16[256,256]{1,0:T(8,128)(2,1)} async-done(((bf16[256,1024]{1,0:T(8,128)(2,1)}), bf16[256,256]{1,0:T(8,128)(2,1)}) %reduce-scatter.5.cloned.1.call-update) | async-done | bytes 131088 | tf_op jit(solution)/shard_map/reduce_scatter | solution.py:129
  157.4 5.8 %all-reduce = (f32[256]{0:T(256)S(1)}, f32[256]{0:T(256)S(1)}) all-reduce(f32[256]{0:T(256)S(1)} %get-tuple-element.5, f32[256]{0:T(256)S(1)} %get-tuple-element.4), channel_id=1, replica_groups=mesh['req'=8,'mdl'=4] {'mdl'}, use_global_device_ids=true, to_apply=%region_14.15 | all-reduce | flops 512 | bytes 4096 | tf_op jit(solution)/shard_map/psum | solution.py:136
  163.2 1.7 add_convert_fusion
  (209 shorter events, 31.5 us)
Async XLA Ops:
  7.2 124.3 %copy-start = (bf16[512,1024]{1,0:T(8,128)(2,1)S(1)}, bf16[512,1024]{1,0:T(8,128)(2,1)}, u32[]{:S(2)}) copy-start(bf16[512,1024]{1,0:T(8,128)(2,1)} %param.34) | copy-start | bytes 3145732
  7.9 9.6 %copy-start.44 = (bf16[256]{0:T(256)(128)(2,1)S(1)}, bf16[256]{0:T(256)(128)(2,1)}, u32[]{:S(2)}) copy-start(bf16[256]{0:T(256)(128)(2,1)} %param.26) | copy-start | bytes 1540
  7.9 9.6 %copy-start.12 = (bf16[1024,256]{1,0:T(8,128)(2,1)S(1)}, bf16[1024,256]{1,0:T(8,128)(2,1)}, u32[]{:S(2)}) copy-start(bf16[1024,256]{1,0:T(8,128)(2,1)} %param.28) | copy-start | bytes 1572868
  7.9 10.0 %copy-start.13 = (bf16[1024,256]{1,0:T(8,128)(2,1)S(1)}, bf16[1024,256]{1,0:T(8,128)(2,1)}, u32[]{:S(2)}) copy-start(bf16[1024,256]{1,0:T(8,128)(2,1)} %param.27) | copy-start | bytes 1572868
  8.6 9.7 %copy-start.16 = (bf16[1024,256]{1,0:T(8,128)(2,1)S(1)}, bf16[1024,256]{1,0:T(8,128)(2,1)}, u32[]{:S(2)}) copy-start(bf16[1024,256]{1,0:T(8,128)(2,1)} %param.25) | copy-start | bytes 1572868
  19.1 15.8 %copy-start.27 = (s32[4,4]{1,0:T(4,128)S(1)}, s32[4,4]{1,0:T(4,128)}, u32[]{:S(2)}) copy-start(s32[4,4]{1,0:T(4,128)} %param.40) | copy-start | bytes 196
  19.1 15.9 %copy-start.2 = (bf16[7,128,256]{2,1,0:T(8,128)(2,1)S(1)}, bf16[7,128,256]{2,1,0:T(8,128)(2,1)}, u32[]{:S(2)}) copy-start(bf16[7,128,256]{2,1,0:T(8,128)(2,1)} %param.38) | copy-start | bytes 1376260
  21.2 46.0 %all-to-all-start = ((bf16[8,32,768]{2,1,0:T(8,128)(2,1)}), bf16[8,32,768]{2,1,0:T(8,128)(2,1)S(1)}, u32[]{:S(2)}, u32[]{:S(2)}) async-start(bf16[8,32,768]{2,1,0:T(8,128)(2,1)} %broadcast_select_fusion), calls=%async_computation | async-start | bytes 786432 | tf_op jit(solution)/shard_map/all_to_all | solution.py:191
  42.4 8.6 %copy-start.33 = (pred[256]{0:T(512)(128)(4,1)S(1)}, pred[256]{0:T(512)(128)(4,1)}, u32[]{:S(2)}) copy-start(pred[256]{0:T(512)(128)(4,1)} %get-tuple-element.59) | copy-start | bytes 772
  42.4 8.6 %copy-start.34 = (pred[256]{0:T(512)(128)(4,1)S(1)}, pred[256]{0:T(512)(128)(4,1)}, u32[]{:S(2)}) copy-start(pred[256]{0:T(512)(128)(4,1)} %get-tuple-element.60) | copy-start | bytes 772
  50.5 19.8 %copy-start.20 = (pred[4,512]{1,0:T(4,128)(4,1)}, pred[4,512]{1,0:T(4,128)(4,1)S(1)}, u32[]{:S(2)}) copy-start(pred[4,512]{1,0:T(4,128)(4,1)S(1)} %iota_compare_fusion.4) | copy-start | bytes 6148
  78.7 8.9 %copy-start.26 = (s32[256]{0:T(256)S(1)}, s32[256]{0:T(256)}, u32[]{:S(2)}) copy-start(s32[256]{0:T(256)} %select_select_fusion) | copy-start | bytes 3076
  78.7 17.2 %copy-start.14 = (bf16[256,1024]{1,0:T(8,128)(2,1)S(1)}, bf16[256,1024]{1,0:T(8,128)(2,1)}, u32[]{:S(2)}) copy-start(bf16[256,1024]{1,0:T(8,128)(2,1)} %param.29) | copy-start | bytes 1572868
  79.2 37.0 %copy-start.5 = (bf16[256,256]{1,0:T(8,128)(2,1)S(1)}, bf16[256,256]{1,0:T(8,128)(2,1)}, u32[]{:S(2)}) copy-start(bf16[256,256]{1,0:T(8,128)(2,1)} %param.23) | copy-start | bytes 393220
  80.6 42.4 %copy-start.28 = (f32[256]{0:T(256)S(1)}, f32[256]{0:T(256)}, u32[]{:S(2)}) copy-start(f32[256]{0:T(256)} %param.31) | copy-start | bytes 3076
  80.6 42.4 %copy-start.29 = (f32[256]{0:T(256)S(1)}, f32[256]{0:T(256)}, u32[]{:S(2)}) copy-start(f32[256]{0:T(256)} %param.30) | copy-start | bytes 3076
  81.4 13.3 %all-to-all-start.1 = ((bf16[8,32,256]{2,1,0:T(8,128)(2,1)}), bf16[8,32,256]{2,1,0:T(8,128)(2,1)S(1)}, u32[]{:S(2)}, u32[]{:S(2)}) async-start(bf16[8,32,256]{2,1,0:T(8,128)(2,1)} %broadcast_select_fusion.1), calls=%async_computation.1 | async-start | bytes 262144 | tf_op jit(solution)/shard_map/all_to_all | solution.py:212
  87.4 28.8 %reduce-scatter.3.cloned.1.call-start = ((), (), s32[]{:S(2)}) async-start(), calls=%async_computation.4 | async-start | bytes 655360 | tf_op jit(solution)/shard_map/reduce_scatter | solution.py:129
  94.7 36.7 %copy-start.41 = (bf16[1024,512]{1,0:T(8,128)(2,1)S(1)}, bf16[1024,512]{1,0:T(8,128)(2,1)}, u32[]{:S(2)}) copy-start(bf16[1024,512]{1,0:T(8,128)(2,1)} %param.32) | copy-start | bytes 3145732
  94.7 36.7 %copy-start.43 = (f32[512]{0:T(512)S(1)}, f32[512]{0:T(512)}, u32[]{:S(2)}) copy-start(f32[512]{0:T(512)} %param.33) | copy-start | bytes 6148
  97.0 59.3 %reduce-scatter.5.cloned.1.call-start = ((), (), s32[]{:S(2)}) async-start(), calls=%async_computation.5 | async-start | bytes 655360 | tf_op jit(solution)/shard_map/reduce_scatter | solution.py:129
  131.5 24.8 %copy-start.24 = (f32[256]{0:T(256)S(1)}, f32[256]{0:T(256)}, u32[]{:S(2)}) copy-start(f32[256]{0:T(256)} %param.35) | copy-start | bytes 3076
  131.5 31.7 %copy-start.30 = (f32[256]{0:T(256)S(1)}, f32[256]{0:T(256)}, u32[]{:S(2)}) copy-start(f32[256]{0:T(256)} %param.37) | copy-start | bytes 3076
  131.5 31.7 %copy-start.31 = (f32[256]{0:T(256)S(1)}, f32[256]{0:T(256)}, u32[]{:S(2)}) copy-start(f32[256]{0:T(256)} %param.36) | copy-start | bytes 3076
  (25 other events, 89.1 us)
Sparse Core Ops, SparseCore 0:
  97.1 19.0 reduce-scatter.2
  134.4 21.9 reduce-scatter.4
where the time goes:
time: 173 us; the launch traced here: 172 us
  waiting for transfers between devices  46.2 us (27%)
  other arithmetic  37.5 us (22%)
  blocking collectives  27.5 us (16%)
  local copies, waits for them, and re-layouts  22.5 us (13%)
  between operations  14.8 us (9%)
  starting transfers between devices  12.1 us (7%)
  matrix products  11.2 us (6%)
    reduce_scatter x2, waiting for transfers between devices, reduce_groups(): lax.psum_scatter(partial_value.astype(jnp.bfloat16), 'mdl', scatter_dimen...  39.1 us
    gather x15, other arithmetic, arriving_rows(): slot_of = inverse[request]  22.7 us
    all_gather x2, blocking collectives, fold_features(): piece = lax.all_gather(row_part, 'mdl', axis=1, tiled=True)  16 us
    psum x2, blocking collectives, normalize(): lax.psum((jnp.sum(hidden, axis=1), jnp.sum(hidden * hidden, axis=1)), 'mdl')  11.5 us
    all_to_all x1, waiting for transfers between devices, per_device(): lax.all_to_all(back, 'req', split_axis=0, concat_axis=0, tiled=True)  7.07 us
    all_to_all x1, starting transfers between devices, per_device(): lax.all_to_all(back, 'req', split_axis=0, concat_axis=0, tiled=True)  5.99 us
    all_to_all x1, starting transfers between devices, per_device(): lax.all_to_all(outgoing, 'req', split_axis=0, concat_axis=0, tiled=True)  5.83 us
  transfers between devices with their start and end apart: 4, of which 3 were waited for; matrix products, arithmetic and copies ran while one was open for 24% of the time, Pallas kernels for 0%

commit v1 on v0

--- a/solution.py
+++ b/solution.py
@@ -1,6 +1,10 @@
+import functools
+
 import jax
 import jax.numpy as jnp
 from jax import lax
+from jax.experimental import pallas as pl
+from jax.experimental.pallas import tpu as pltpu
 from jax.sharding import PartitionSpec as P
 
 HD = 64
@@ -143,7 +147,7 @@
     ).astype(jnp.bfloat16)
 
 
-def per_device(
+def per_device_general(
     tokens,
     perm,
     w_query,
@@ -223,6 +227,480 @@
     return (layer_out, kept_keys, kept_values)
 
 
+MESH = pl.DeviceIdType.MESH
+NT = (((1,), (1,)), ((), ()))
+
+
+def mm(left, right):
+    return jnp.dot(left, right, preferred_element_type=jnp.float32)
+
+
+def iota(shape, axis):
+    return lax.broadcasted_iota(jnp.int32, shape, axis)
+
+
+def fused_kernel(
+    pages_dev,
+    perm_ref,
+    page_ref,
+    len_ref,
+    accepted_ref,
+    parents_ref,
+    q_bias_ref,
+    gain1_ref,
+    bias1_ref,
+    fc1_bias_ref,
+    fc2_bias_ref,
+    gain2_ref,
+    bias2_ref,
+    tokens_hbm,
+    wq_hbm,
+    wk_hbm,
+    wv_hbm,
+    wo_hbm,
+    w1_hbm,
+    w2_hbm,
+    keys_hbm,
+    values_hbm,
+    out_ref,
+    kept_k_ref,
+    kept_v_ref,
+    tokens_v,
+    wq_v,
+    wk_v,
+    wv_v,
+    wo_v,
+    w1_v,
+    w2_v,
+    keys_v,
+    values_v,
+    onehot_f,
+    send1,
+    recv1,
+    x_all,
+    params,
+    acc_ref,
+    q_ref,
+    k_ref,
+    v_ref,
+    anc_ref,
+    part_ref,
+    recv2,
+    nf_all,
+    ff_ref,
+    recv3,
+    send5,
+    recv5,
+    load_sem,
+    ssem1,
+    rsem1,
+    ssem_x,
+    rsem_x,
+    ssem_p,
+    rsem_p,
+    ssem2,
+    rsem2,
+    ssem_n,
+    rsem_n,
+    ssem3,
+    rsem3,
+    ssem5,
+    rsem5,
+):
+    n_req = lax.axis_size("req")
+    n_mdl = lax.axis_size("mdl")
+    r = lax.axis_index("req")
+    m = lax.axis_index("mdl")
+    requests = perm_ref.shape[0]
+    rows, width = tokens_v.shape
+    draft = parents_ref.shape[1]
+    per_dev = parents_ref.shape[0]
+    pos_dev = rows // requests
+    full = width * n_mdl
+
+    core = m + 1 - 2 * (m % 2)
+    across = (m + 2) % n_mdl
+    diag = (core + 2) % n_mdl
+    peers = (diag, across, core)
+
+    loads = []
+    for i, (source, target) in enumerate(
+        (
+            (tokens_hbm, tokens_v),
+            (wq_hbm, wq_v),
+            (wk_hbm, wk_v),
+            (wv_hbm, wv_v),
+            (keys_hbm, keys_v),
+            (values_hbm, values_v),
+            (wo_hbm, wo_v),
+            (w1_hbm, w1_v),
+            (w2_hbm, w2_v),
+        )
+    ):
+        copy = pltpu.make_async_copy(source, target, load_sem.at[i])
+        copy.start()
+        loads.append(copy)
+
+    barrier = pltpu.get_barrier_semaphore()
+    others = [(i, j) for i in range(n_req) for j in range(n_mdl) if (i, j) != (0, 0)]
+    for i, j in others:
+        pl.semaphore_signal(
+            barrier,
+            inc=1,
+            device_id=((r + i) % n_req, (m + j) % n_mdl),
+            device_id_type=MESH,
+        )
+
+    block = (pos_dev, rows)
+    place = iota(block, 1) - iota(block, 0) * requests
+    for s in range(requests):
+        onehot_f[s * pos_dev : (s + 1) * pos_dev, :] = (place == perm_ref[s]).astype(jnp.float32)
+    onehot = onehot_f[...]
+    loads[0].wait()
+    packed = mm(onehot.astype(jnp.bfloat16), tokens_v[...]).astype(jnp.bfloat16)
+    send1[...] = packed.reshape(send1.shape)
+
+    params[m, 0:1, :] = gain1_ref[...]
+    params[m, 1:2, :] = bias1_ref[...]
+    params[m, 2:3, :] = fc2_bias_ref[...]
+    params[m, 3:4, :] = gain2_ref[...]
+    params[m, 4:5, :] = bias2_ref[...]
+    params[m, 5:8, :] = jnp.zeros((3, width), jnp.float32)
+
+    pl.semaphore_wait(barrier, len(others))
+
+    copies1 = []
+    for i in range(1, n_req):
+        to = (r + i) % n_req
+        copy = pltpu.make_async_remote_copy(
+            src_ref=send1.at[to],
+            dst_ref=recv1.at[r],
+            send_sem=ssem1.at[i],
+            recv_sem=rsem1.at[i],
+            device_id=(to, m),
+            device_id_type=MESH,
+        )
+        copy.start()
+        copies1.append(copy)
+    recv1[r] = send1[r]
+
+    def push(source, target, ssem, rsem, i):
+        copy = pltpu.make_async_remote_copy(
+            src_ref=source,
+            dst_ref=target,
+            send_sem=ssem.at[i],
+            recv_sem=rsem.at[i],
+            device_id=(r, peers[i]),
+            device_id_type=MESH,
+        )
+        copy.start()
+        return copy
+
+    copies_p = [push(params.at[m], params.at[m], ssem_p, rsem_p, i) for i in range(3)]
+
+    square = (draft, draft)
+    row_id, col_id = iota(square, 0), iota(square, 1)
+    hops, reach = [], []
+    for b in range(per_dev):
+        line = jnp.broadcast_to(parents_ref[b : b + 1, :], square)
+        column = jnp.sum(jnp.where(row_id == col_id, line, 0), axis=1, keepdims=True)
+        hops.append((column == col_id).astype(jnp.bfloat16))
+        reach.append((row_id == col_id).astype(jnp.float32))
+    steps = (draft - 1).bit_length()
+    for step in range(steps):
+        for b in range(per_dev):
+            hop = hops[b]
+            reach[b] = jnp.minimum(reach[b] + mm(reach[b].astype(jnp.bfloat16), hop), 1.0)
+            if step < steps - 1:
+                hops[b] = jnp.minimum(mm(hop, hop), 1.0).astype(jnp.bfloat16)
+    for b in range(per_dev):
+        anc_ref[b] = reach[b]
+
+    big = (rows, rows)
+    n_id, c_id = iota(big, 0), iota(big, 1)
+    lane, pos = n_id // draft, n_id % draft
+    arrival = (pos // pos_dev) * (per_dev * pos_dev) + lane * pos_dev + pos % pos_dev
+    reorder = (c_id == arrival).astype(jnp.float32).astype(jnp.bfloat16)
+    home = jnp.transpose(onehot).astype(jnp.bfloat16)
+
+    for copy in copies1:
+        copy.wait()
+    x_own = mm(reorder, recv1[...].reshape(rows, width)).astype(jnp.bfloat16)
+    x_all[m] = x_own
+    copies_x = [push(x_all.at[m], x_all.at[m], ssem_x, rsem_x, i) for i in range(3)]
+
+    for i in (1, 2, 3):
+        loads[i].wait()
+
+    def project(which, first):
+        part = x_all[which]
+        span = pl.ds(pl.multiple_of(which * width, width), width)
+        for j, weight in enumerate((wq_v, wk_v, wv_v)):
+            value = mm(part, weight[span, :])
+            if first:
+                acc_ref[j] = value
+            else:
+                acc_ref[j] += value
+
+    project(m, True)
+    for i in (2, 1, 0):
+        copies_x[i].wait()
+        project(peers[i], False)
+    q_ref[...] = (acc_ref[0] + q_bias_ref[...].astype(jnp.float32)).astype(jnp.bfloat16)
+    k_ref[...] = acc_ref[1].astype(jnp.bfloat16)
+    v_ref[...] = acc_ref[2].astype(jnp.bfloat16)
+
+    for i in (4, 5, 6):
+        loads[i].wait()
+
+    heads = width // HD
+    page_len = keys_v.shape[1]
+    max_pages = page_ref.shape[1]
+    head_lane = iota((draft, width), 1) // HD
+    head_masks = [
+        (head_lane == h).astype(jnp.float32).astype(jnp.bfloat16) for h in range(heads)
+    ]
+    key_id = iota((heads * draft, page_len), 1)
+    scale = HD ** (-0.5)
+
+    def attend_slot(b):
+        span = pl.ds(pl.multiple_of(b * draft, draft), draft)
+        slot_query = q_ref[span, :]
+        stacked = jnp.concatenate([slot_query * mask for mask in head_masks], axis=0)
+        length = len_ref[b]
+        scores, values = [], []
+        for t in range(max_pages):
+            page = lax.rem(page_ref[b, t], pages_dev)
+            part = lax.dot_general(stacked, keys_v[page], NT, preferred_element_type=jnp.float32)
+            scores.append(jnp.where(key_id < length - t * page_len, part * scale, -1e30))
+            values.append(values_v[page])
+        part = lax.dot_general(stacked, k_ref[span, :], NT, preferred_element_type=jnp.float32)
+        tree = jnp.concatenate([anc_ref[b]] * heads, axis=0)
+        scores.append(jnp.where(tree > 0.5, part * scale, -1e30))
+        values.append(v_ref[span, :])
+        peak = functools.reduce(jnp.maximum, scores[:-1])
+        peak = jnp.maximum(
+            jnp.max(peak, axis=1, keepdims=True), jnp.max(scores[-1], axis=1, keepdims=True)
+        )
+        weights = [jnp.exp(part - peak) for part in scores]
+        total = jnp.sum(sum(weights[1:-1], weights[0]), axis=1, keepdims=True)
+        total = total + jnp.sum(weights[-1], axis=1, keepdims=True)
+        inverse = 1.0 / total
+        mixed = sum(
+            mm((weight * inverse).astype(jnp.bfloat16), value)
+            for weight, value in zip(weights, values)
+        )
+        result = jnp.zeros((draft, width), jnp.float32)
+        for h in range(heads):
+            result = jnp.where(head_lane == h, mixed[h * draft : (h + 1) * draft], result)
+        return result.astype(jnp.bfloat16)
+
+    copies2 = []
+    for i, b in enumerate(peers):
+        part_ref[b] = mm(attend_slot(b), wo_v[...]).astype(jnp.bfloat16)
+        copies2.append(push(part_ref.at[b], recv2.at[m], ssem2, rsem2, i))
+    recv2[m] = mm(attend_slot(m), wo_v[...]).astype(jnp.bfloat16)
+
+    count = accepted_ref.shape[1]
+    for b in range(per_dev):
+        pick_row, pick_col = iota((count, rows), 0), iota((count, rows), 1)
+        wanted = jnp.zeros((count, rows), jnp.int32)
+        for a in range(count):
+            wanted = jnp.where(pick_row == a, accepted_ref[b, a] + b * draft, wanted)
+        pick = (pick_col == wanted).astype(jnp.float32).astype(jnp.bfloat16)
+        kept_k_ref[b] = mm(pick, k_ref[...]).astype(jnp.bfloat16)
+        kept_v_ref[b] = mm(pick, v_ref[...]).astype(jnp.bfloat16)
+
+    for copy in copies_p:
+        copy.wait()
+
+    def vector(row):
+        return jnp.concatenate([params[g, row : row + 1, :] for g in range(n_mdl)], axis=1)
+
+    def layer_norm(hidden, gain, bias):
+        mean = jnp.sum(hidden, axis=1, keepdims=True) / full
+        var = jnp.sum(hidden * hidden, axis=1, keepdims=True) / full - mean * mean
+        return (hidden - mean) * lax.rsqrt(var + 1e-05) * gain + bias
+
+    own = pl.ds(pl.multiple_of(m * draft, draft), draft)
+    hidden = jnp.concatenate([x_all[g, own, :] for g in range(n_mdl)], axis=1).astype(jnp.float32)
+    for copy in copies2:
+        copy.wait()
+    for g in range(n_mdl):
+        hidden = hidden + recv2[g].astype(jnp.float32)
+    normed = layer_norm(hidden, vector(0), vector(1)).astype(jnp.bfloat16)
+    nf_all[m] = normed
+    copies_n = [push(nf_all.at[m], nf_all.at[m], ssem_n, rsem_n, i) for i in range(3)]
+    loads[7].wait()
+    loads[8].wait()
+
+    def feed(pair):
+        start = pl.multiple_of(pair * 2, 2)
+        part = nf_all[pl.ds(start, 2)].reshape(2 * draft, full)
+        inner = mm(part, w1_v[...]) + fc1_bias_ref[...]
+        active = (0.5 * inner * (1.0 + lax.erf(inner * (0.5**0.5)))).astype(jnp.bfloat16)
+        result = mm(active, w2_v[...]).astype(jnp.bfloat16)
+        ff_ref[pl.ds(start, 2)] = result.reshape(2, draft, full)
+
+    copies_n[2].wait()
+    feed(m // 2)
+    copies3 = [None] * 3
+    copies3[2] = push(ff_ref.at[core], recv3.at[m], ssem3, rsem3, 2)
+    copies_n[1].wait()
+    copies_n[0].wait()
+    feed(1 - m // 2)
+    for i in (0, 1):
+        copies3[i] = push(ff_ref.at[peers[i]], recv3.at[m], ssem3, rsem3, i)
+    recv3[m] = ff_ref[m]
+    second = normed.astype(jnp.float32) + vector(2)
+    for copy in (copies3[2], copies3[1], copies3[0]):
+        copy.wait()
+    for g in range(n_mdl):
+        second = second + recv3[g].astype(jnp.float32)
+    final = layer_norm(second, vector(3), vector(4))
+    for t in range(n_req):
+        for g in range(n_mdl):
+            send5[t, g] = final[
+                t * pos_dev : (t + 1) * pos_dev, g * width : (g + 1) * width
+            ].astype(jnp.bfloat16)
+    me = r * n_mdl + m
+    copies5 = []
+    for n, (i, j) in enumerate(others):
+        to_r, to_m = (r + i) % n_req, (m + j) % n_mdl
+        copy = pltpu.make_async_remote_copy(
+            src_ref=send5.at[to_r, to_m],
+            dst_ref=recv5.at[me],
+            send_sem=ssem5.at[n],
+            recv_sem=rsem5.at[n],
+            device_id=(to_r, to_m),
+            device_id_type=MESH,
+        )
+        copy.start()
+        copies5.append(copy)
+    recv5[me] = send5[r, m]
+    for copy in copies5:
+        copy.wait()
+    arrived = recv5[...].astype(jnp.float32).reshape(rows, width).astype(jnp.bfloat16)
+    out_ref[...] = mm(home, arrived).astype(jnp.bfloat16)
+
+
+def per_device_fused(
+    tokens,
+    perm,
+    w_query,
+    q_bias,
+    w_key,
+    w_value,
+    w_out,
+    norm_gain,
+    norm_bias,
+    w_fc1,
+    fc1_bias,
+    w_fc2,
+    fc2_bias,
+    final_gain,
+    final_bias,
+    key_pool,
+    value_pool,
+    page_table,
+    cache_len,
+    parents,
+    accepted,
+):
+    n_req = lax.axis_size("req")
+    n_mdl = lax.axis_size("mdl")
+    rows, width = tokens.shape
+    per_dev, draft = parents.shape
+    full = width * n_mdl
+    pos_dev = rows // perm.shape[0]
+    smem = pl.BlockSpec(memory_space=pltpu.SMEM)
+    vmem = pl.BlockSpec(memory_space=pltpu.VMEM)
+    hbm = pl.BlockSpec(memory_space=pltpu.HBM)
+    bf16, f32 = jnp.bfloat16, jnp.float32
+    large = (tokens, w_query, w_key, w_value, w_out, w_fc1, w_fc2, key_pool, value_pool)
+    n_all = n_req * n_mdl
+    dma = pltpu.SemaphoreType.DMA
+    kept = jax.ShapeDtypeStruct((per_dev, accepted.shape[1], width), bf16)
+    return tuple(
+        pl.pallas_call(
+            functools.partial(fused_kernel, key_pool.shape[0]),
+            out_shape=(jax.ShapeDtypeStruct((rows, width), bf16), kept, kept),
+            in_specs=[smem] * 4 + [vmem] * 8 + [hbm] * 9,
+            out_specs=(vmem, vmem, vmem),
+            scratch_shapes=[pltpu.VMEM(a.shape, a.dtype) for a in large]
+            + [
+                pltpu.VMEM((rows, rows), f32),
+                pltpu.VMEM((n_req, rows // n_req, width), bf16),
+                pltpu.VMEM((n_req, rows // n_req, width), bf16),
+                pltpu.VMEM((n_mdl, rows, width), bf16),
+                pltpu.VMEM((n_mdl, 8, width), f32),
+                pltpu.VMEM((3, rows, width), f32),
+                pltpu.VMEM((rows, width), bf16),
+                pltpu.VMEM((rows, width), bf16),
+                pltpu.VMEM((rows, width), bf16),
+                pltpu.VMEM((per_dev, draft, draft), f32),
+                pltpu.VMEM((n_mdl, draft, full), bf16),
+                pltpu.VMEM((n_mdl, draft, full), bf16),
+                pltpu.VMEM((n_mdl, draft, full), bf16),
+                pltpu.VMEM((n_mdl, draft, full), bf16),
+                pltpu.VMEM((n_mdl, draft, full), bf16),
+                pltpu.VMEM((n_req, n_mdl, pos_dev, width), bf16),
+                pltpu.VMEM((n_all, pos_dev, width), bf16),
+                dma((9,)),
+                dma((n_req,)),
+                dma((n_req,)),
+                dma((3,)),
+                dma((3,)),
+                dma((3,)),
+                dma((3,)),
+                dma((3,)),
+                dma((3,)),
+                dma((3,)),
+                dma((3,)),
+                dma((3,)),
+                dma((3,)),
+                dma((n_all,)),
+                dma((n_all,)),
+            ],
+            compiler_params=pltpu.CompilerParams(
+                collective_id=0, has_side_effects=True, vmem_limit_bytes=56 * 2**20
+            ),
+        )(
+            perm,
+            page_table,
+            cache_len,
+            accepted,
+            parents,
+            q_bias[None, :],
+            norm_gain[None, :],
+            norm_bias[None, :],
+            fc1_bias[None, :],
+            fc2_bias[None, :],
+            final_gain[None, :],
+            final_bias[None, :],
+            tokens,
+            w_query,
+            w_key,
+            w_value,
+            w_out,
+            w_fc1,
+            w_fc2,
+            key_pool,
+            value_pool,
+        )
+    )
+
+
+def per_device(*args):
+    rows, requests = args[0].shape[0], args[1].shape[0]
+    per_dev, draft = args[19].shape
+    n_mdl = lax.axis_size("mdl")
+    whole_positions = rows % requests == 0 and rows // requests == 8
+    if whole_positions and per_dev == n_mdl == 4 and per_dev * draft == rows:
+        return per_device_fused(*args)
+    return per_device_general(*args)
+
+
 def solution(mesh):
     in_specs = (
         P("req", "mdl"),

time: 173 us -> 52.7 us (0.30)
  Pallas kernels: 0 us -> 47.6 us
  waiting for transfers between devices: 46.2 us -> 0 us
  other arithmetic: 37.5 us -> 0 us
  blocking collectives: 27.5 us -> 0 us
  local copies, waits for them, and re-layouts: 22.5 us -> 4.12 us
  between operations: 14.8 us -> 0.66 us
  starting transfers between devices: 12.1 us -> 0 us
  matrix products: 11.2 us -> 0 us
    pallas_call x0 -> x1, Pallas kernels: none -> 47.6 us  [per_device_fused(): pl.pallas_call(functools.partial(fused_kernel, key_pool.shape[0]), out_sh...]
    reduce_scatter x2 -> x0, waiting for transfers between devices: 39.1 us -> none  [reduce_groups(): lax.psum_scatter(partial_value.astype(jnp.bfloat16), 'mdl', scatter_dimen...]
    gather x24 -> x0, other arithmetic: 24 us -> none  [the longest x15 22.7 us: arriving_rows(): slot_of = inverse[request]]
    all_gather x2 -> x0, blocking collectives: 16 us -> none  [fold_features(): piece = lax.all_gather(row_part, 'mdl', axis=1, tiled=True)]
    gather x16 -> x0, local copies, waits for them, and re-layouts: 13.3 us -> none  [the longest x2 1.69 us: attend(): key_pool[local_pages].reshape(per_dev, -1, head_count, HD)]
    all_to_all x2 -> x0, starting transfers between devices: 11.8 us -> none  [the longest x1 5.99 us: per_device(): lax.all_to_all(back, 'req', split_axis=0, concat_axis=0, tiled=True)]
    psum x2 -> x0, blocking collectives: 11.5 us -> none  [normalize(): lax.psum((jnp.sum(hidden, axis=1), jnp.sum(hidden * hidden, axis=1)), 'mdl')]
    dot_general x19 -> x0, matrix products: 11.2 us -> none  [the longest x1 2.7 us: per_device(): jnp.dot(activated, w_fc2, preferred_element_type=jnp.float32)]
  transfers between devices with their start and end apart: 4 -> 0, of which waited for: 3 -> 0; matrix products, arithmetic and copies ran while one was open for 24% -> 0% of each run, Pallas kernels for 0% -> 0%
where the time goes in v1:
time: 52.7 us; the launch traced here: 52.4 us
  Pallas kernels  47.6 us (90%)
  local copies, waits for them, and re-layouts  4.12 us (8%)
  between operations  0.66 us (1%)
    pallas_call x1, Pallas kernels, per_device_fused(): pl.pallas_call(functools.partial(fused_kernel, key_pool.shape[0]), out_sh...  47.6 us
    unnamed x9, local copies, waits for them, and re-layouts  3.55 us

profile of v1, /device:TPU:0, one launch (start us, length us, event | category | flops | bytes accessed | tf_op | source)
XLA Modules:
  0.0 52.4 jit_solution(6892856472715973291)
XLA Ops:
  0.6 0.0 copy-start.2
  0.6 0.6 %copy-done.2 = bf16[256]{0:T(256)(128)(2,1)S(1)} copy-done((bf16[256]{0:T(256)(128)(2,1)S(1)}, bf16[256]{0:T(256)(128)(2,1)}, u32[]{:S(2)}) %copy-start.2) | copy-done | bytes 536
  1.3 0.6 %broadcast_in_dim.21.q_bias_ref = bf16[1,256]{1,0:T(2,128)(2,1)} reshape(bf16[256]{0:T(256)(128)(2,1)S(1)} %copy-done.2) | data formatting | bytes 1024 | tf_op jit(solution)/shard_map/broadcast_in_dim | solution.py:674
  1.9 47.6 %shard_map.220 = (bf16[256,256]{1,0:T(8,128)(2,1)}, bf16[4,8,256]{2,1,0:T(8,128)(2,1)}, bf16[4,8,256]{2,1,0:T(8,128)(2,1)}) custom-call(s32[32]{0:T(128)} %perm_ref.1, s32[4,4]{1,0:T(4,128)} %page_ref.1, s32[4]{0:T(128)} %len_ref.1, s32[4,8]{1,0:T(4,128)} %accepted_ref.1, s32[4,64]{1,0:T(4,128)} %parents_ref.1, bf16[1,256]{1,0:T(2,128)(2,1)} %broadcast_in_dim.21.q_bias_ref, ...), custom_call_target="tpu_custom_call" | custom-call | tf_op jit(solution)/shard_map/pallas_call | solution.py:625
  49.5 0.0 copy-start.1
  49.5 1.6 %copy.27 = bf16[256,256]{1,0:T(8,128)(2,1)} copy(bf16[256,256]{1,0:T(8,128)(2,1)} %get-tuple-element.6) | data formatting | bytes 262144
  51.1 0.0 copy-done.1
  51.1 0.0 copy-start
  51.1 0.6 %copy.28 = bf16[4,8,256]{2,1,0:T(8,128)(2,1)} copy(bf16[4,8,256]{2,1,0:T(8,128)(2,1)S(1)} %copy-done.1) | data formatting | bytes 32768
  51.7 0.1 copy-done
  51.8 0.6 %copy.29 = bf16[4,8,256]{2,1,0:T(8,128)(2,1)} copy(bf16[4,8,256]{2,1,0:T(8,128)(2,1)S(1)} %copy-done) | data formatting | bytes 32768
Async XLA Ops:
  0.6 0.7 %copy-start.2 = (bf16[256]{0:T(256)(128)(2,1)S(1)}, bf16[256]{0:T(256)(128)(2,1)}, u32[]{:S(2)}) copy-start(bf16[256]{0:T(256)(128)(2,1)} %param.24) | copy-start | bytes 1540
  49.5 1.6 %copy-start.1 = (bf16[4,8,256]{2,1,0:T(8,128)(2,1)S(1)}, bf16[4,8,256]{2,1,0:T(8,128)(2,1)}, u32[]{:S(2)}) copy-start(bf16[4,8,256]{2,1,0:T(8,128)(2,1)} %get-tuple-element.7) | copy-start | bytes 49156
  51.1 0.7 %copy-start = (bf16[4,8,256]{2,1,0:T(8,128)(2,1)S(1)}, bf16[4,8,256]{2,1,0:T(8,128)(2,1)}, u32[]{:S(2)}) copy-start(bf16[4,8,256]{2,1,0:T(8,128)(2,1)} %get-tuple-element.8) | copy-start | bytes 49156

commit v2 on v1

--- a/solution.py
+++ b/solution.py
@@ -276,7 +276,6 @@
     values_v,
     onehot_f,
     send1,
-    recv1,
     x_all,
     params,
     acc_ref,
@@ -288,6 +287,7 @@
     recv2,
     nf_all,
     ff_ref,
+    part3,
     recv3,
     send5,
     recv5,
@@ -322,6 +322,16 @@
     across = (m + 2) % n_mdl
     diag = (core + 2) % n_mdl
     peers = (diag, across, core)
+    half = n_req // 2
+
+    def place(source):
+        return source % 2 * half + source // 2
+
+    def position(row):
+        group = row // pos_dev
+        return (group % half * 2 + group // half) * pos_dev + row % pos_dev
+
+    spot = place(r)
 
     loads = []
     for i, (source, target) in enumerate(
@@ -342,7 +352,7 @@
         loads.append(copy)
 
     barrier = pltpu.get_barrier_semaphore()
-    others = [(i, j) for i in range(n_req) for j in range(n_mdl) if (i, j) != (0, 0)]
+    others = [(i, 0) for i in range(1, n_req)] + [(0, j) for j in range(1, n_mdl)]
     for i, j in others:
         pl.semaphore_signal(
             barrier,
@@ -352,13 +362,13 @@
         )
 
     block = (pos_dev, rows)
-    place = iota(block, 1) - iota(block, 0) * requests
+    local = iota(block, 1) - iota(block, 0) * requests
     for s in range(requests):
-        onehot_f[s * pos_dev : (s + 1) * pos_dev, :] = (place == perm_ref[s]).astype(jnp.float32)
+        onehot_f[s * pos_dev : (s + 1) * pos_dev, :] = (local == perm_ref[s]).astype(jnp.float32)
     onehot = onehot_f[...]
     loads[0].wait()
-    packed = mm(onehot.astype(jnp.bfloat16), tokens_v[...]).astype(jnp.bfloat16)
-    send1[...] = packed.reshape(send1.shape)
+    packed = mm(onehot.astype(jnp.bfloat16), tokens_v[...])
+    send1[...] = packed.reshape(send1.shape).astype(jnp.bfloat16)
 
     params[m, 0:1, :] = gain1_ref[...]
     params[m, 1:2, :] = bias1_ref[...]
@@ -369,12 +379,13 @@
 
     pl.semaphore_wait(barrier, len(others))
 
+    order = (1, n_req - 1, 2, n_req - 2, 3, n_req - 3, half)
     copies1 = []
-    for i in range(1, n_req):
+    for i in order:
         to = (r + i) % n_req
         copy = pltpu.make_async_remote_copy(
             src_ref=send1.at[to],
-            dst_ref=recv1.at[r],
+            dst_ref=x_all.at[m, :, spot],
             send_sem=ssem1.at[i],
             recv_sem=rsem1.at[i],
             device_id=(to, m),
@@ -382,29 +393,32 @@
         )
         copy.start()
         copies1.append(copy)
-    recv1[r] = send1[r]
-
-    def push(source, target, ssem, rsem, i):
+    x_all[m, :, spot] = send1[r]
+
+    def push(source, target, ssem, rsem, i, peer):
         copy = pltpu.make_async_remote_copy(
             src_ref=source,
             dst_ref=target,
             send_sem=ssem.at[i],
             recv_sem=rsem.at[i],
-            device_id=(r, peers[i]),
+            device_id=(r, peer),
             device_id_type=MESH,
         )
         copy.start()
         return copy
 
-    copies_p = [push(params.at[m], params.at[m], ssem_p, rsem_p, i) for i in range(3)]
+    copies_p = [
+        push(params.at[m], params.at[m], ssem_p, rsem_p, i, peer) for i, peer in enumerate(peers)
+    ]
 
     square = (draft, draft)
     row_id, col_id = iota(square, 0), iota(square, 1)
+    row_pos, col_pos = position(row_id), position(col_id)
     hops, reach = [], []
     for b in range(per_dev):
         line = jnp.broadcast_to(parents_ref[b : b + 1, :], square)
-        column = jnp.sum(jnp.where(row_id == col_id, line, 0), axis=1, keepdims=True)
-        hops.append((column == col_id).astype(jnp.bfloat16))
+        column = jnp.sum(jnp.where(row_pos == col_id, line, 0), axis=1, keepdims=True)
+        hops.append((column == col_pos).astype(jnp.bfloat16))
         reach.append((row_id == col_id).astype(jnp.float32))
     steps = (draft - 1).bit_length()
     for step in range(steps):
@@ -416,24 +430,23 @@
     for b in range(per_dev):
         anc_ref[b] = reach[b]
 
-    big = (rows, rows)
-    n_id, c_id = iota(big, 0), iota(big, 1)
-    lane, pos = n_id // draft, n_id % draft
-    arrival = (pos // pos_dev) * (per_dev * pos_dev) + lane * pos_dev + pos % pos_dev
-    reorder = (c_id == arrival).astype(jnp.float32).astype(jnp.bfloat16)
     home = jnp.transpose(onehot).astype(jnp.bfloat16)
 
-    for copy in copies1:
-        copy.wait()
-    x_own = mm(reorder, recv1[...].reshape(rows, width)).astype(jnp.bfloat16)
-    x_all[m] = x_own
-    copies_x = [push(x_all.at[m], x_all.at[m], ssem_x, rsem_x, i) for i in range(3)]
+    far_x = []
+    for i, copy in zip((0,) + order, [None] + copies1):
+        if copy is not None:
+            copy.wait_recv()
+        piece = place((r + n_req - i) % n_req)
+        far_x.append(
+            push(x_all.at[m, :, piece], x_all.at[m, :, piece], ssem_x, rsem_x, i, across)
+        )
+    near_x = push(x_all.at[m], x_all.at[m], ssem_x, rsem_x, n_req, core)
 
     for i in (1, 2, 3):
         loads[i].wait()
 
     def project(which, first):
-        part = x_all[which]
+        part = x_all[which].astype(jnp.float32).reshape(rows, width).astype(jnp.bfloat16)
         span = pl.ds(pl.multiple_of(which * width, width), width)
         for j, weight in enumerate((wq_v, wk_v, wv_v)):
             value = mm(part, weight[span, :])
@@ -443,9 +456,16 @@
                 acc_ref[j] += value
 
     project(m, True)
-    for i in (2, 1, 0):
-        copies_x[i].wait()
-        project(peers[i], False)
+    for copy in far_x:
+        copy.wait()
+    passed_x = push(x_all.at[across], x_all.at[across], ssem_x, rsem_x, n_req + 1, core)
+    near_x.wait()
+    project(core, False)
+    project(across, False)
+    passed_x.wait()
+    project(diag, False)
+    for copy in copies1:
+        copy.wait_send()
     q_ref[...] = (acc_ref[0] + q_bias_ref[...].astype(jnp.float32)).astype(jnp.bfloat16)
     k_ref[...] = acc_ref[1].astype(jnp.bfloat16)
     v_ref[...] = acc_ref[2].astype(jnp.bfloat16)
@@ -495,18 +515,26 @@
             result = jnp.where(head_lane == h, mixed[h * draft : (h + 1) * draft], result)
         return result.astype(jnp.bfloat16)
 
-    copies2 = []
-    for i, b in enumerate(peers):
-        part_ref[b] = mm(attend_slot(b), wo_v[...]).astype(jnp.bfloat16)
-        copies2.append(push(part_ref.at[b], recv2.at[m], ssem2, rsem2, i))
-    recv2[m] = mm(attend_slot(m), wo_v[...]).astype(jnp.bfloat16)
+    part_ref[0] = mm(attend_slot(diag), wo_v[...]).astype(jnp.bfloat16)
+    mid2 = push(part_ref.at[0], recv2.at[0], ssem2, rsem2, 0, core)
+    share = mm(attend_slot(across), wo_v[...])
+    mid2.wait()
+    part_ref[1] = (share + recv2[0].astype(jnp.float32)).astype(jnp.bfloat16)
+    far2 = push(part_ref.at[1], recv2.at[1], ssem2, rsem2, 1, across)
+    part_ref[2] = mm(attend_slot(core), wo_v[...]).astype(jnp.bfloat16)
+    near2 = push(part_ref.at[2], recv2.at[2], ssem2, rsem2, 2, core)
+    own_part = mm(attend_slot(m), wo_v[...]).astype(jnp.bfloat16).astype(jnp.float32)
 
     count = accepted_ref.shape[1]
+
+    def slot_row(draft_pos):
+        return place(draft_pos // pos_dev) * pos_dev + draft_pos % pos_dev
+
     for b in range(per_dev):
         pick_row, pick_col = iota((count, rows), 0), iota((count, rows), 1)
         wanted = jnp.zeros((count, rows), jnp.int32)
         for a in range(count):
-            wanted = jnp.where(pick_row == a, accepted_ref[b, a] + b * draft, wanted)
+            wanted = jnp.where(pick_row == a, slot_row(accepted_ref[b, a]) + b * draft, wanted)
         pick = (pick_col == wanted).astype(jnp.float32).astype(jnp.bfloat16)
         kept_k_ref[b] = mm(pick, k_ref[...]).astype(jnp.bfloat16)
         kept_v_ref[b] = mm(pick, v_ref[...]).astype(jnp.bfloat16)
@@ -522,64 +550,108 @@
         var = jnp.sum(hidden * hidden, axis=1, keepdims=True) / full - mean * mean
         return (hidden - mean) * lax.rsqrt(var + 1e-05) * gain + bias
 
-    own = pl.ds(pl.multiple_of(m * draft, draft), draft)
-    hidden = jnp.concatenate([x_all[g, own, :] for g in range(n_mdl)], axis=1).astype(jnp.float32)
-    for copy in copies2:
-        copy.wait()
-    for g in range(n_mdl):
-        hidden = hidden + recv2[g].astype(jnp.float32)
+    hidden = jnp.concatenate(
+        [x_all[g, m].astype(jnp.float32).reshape(draft, width) for g in range(n_mdl)], axis=1
+    )
+    hidden = hidden + own_part
+    near2.wait()
+    hidden = hidden + recv2[2].astype(jnp.float32)
+    far2.wait()
+    hidden = hidden + recv2[1].astype(jnp.float32)
     normed = layer_norm(hidden, vector(0), vector(1)).astype(jnp.bfloat16)
-    nf_all[m] = normed
-    copies_n = [push(nf_all.at[m], nf_all.at[m], ssem_n, rsem_n, i) for i in range(3)]
+    rows_k = draft // 2
+    for k in range(2):
+        nf_all[k, m] = normed[k * rows_k : (k + 1) * rows_k]
+    far_n = [push(nf_all.at[k, m], nf_all.at[k, m], ssem_n, rsem_n, k, across) for k in range(2)]
+    near_n = [push(nf_all.at[k, m], nf_all.at[k, m], ssem_n, rsem_n, 2 + k, core) for k in range(2)]
+    passed_n = []
     loads[7].wait()
     loads[8].wait()
-
-    def feed(pair):
+    second = normed.astype(jnp.float32) + vector(2)
+    second = [second[:rows_k], second[rows_k:]]
+
+    def pass_on(k):
+        far_n[k].wait()
+        block = nf_all.at[k, across]
+        passed_n.append(push(block, block, ssem_n, rsem_n, 4 + k, core))
+
+    def feed(k, pair):
         start = pl.multiple_of(pair * 2, 2)
-        part = nf_all[pl.ds(start, 2)].reshape(2 * draft, full)
+        part = nf_all[k, pl.ds(start, 2)].reshape(2 * rows_k, full)
         inner = mm(part, w1_v[...]) + fc1_bias_ref[...]
         active = (0.5 * inner * (1.0 + lax.erf(inner * (0.5**0.5)))).astype(jnp.bfloat16)
-        result = mm(active, w2_v[...]).astype(jnp.bfloat16)
-        ff_ref[pl.ds(start, 2)] = result.reshape(2, draft, full)
-
-    copies_n[2].wait()
-    feed(m // 2)
-    copies3 = [None] * 3
-    copies3[2] = push(ff_ref.at[core], recv3.at[m], ssem3, rsem3, 2)
-    copies_n[1].wait()
-    copies_n[0].wait()
-    feed(1 - m // 2)
-    for i in (0, 1):
-        copies3[i] = push(ff_ref.at[peers[i]], recv3.at[m], ssem3, rsem3, i)
-    recv3[m] = ff_ref[m]
-    second = normed.astype(jnp.float32) + vector(2)
-    for copy in (copies3[2], copies3[1], copies3[0]):
-        copy.wait()
-    for g in range(n_mdl):
-        second = second + recv3[g].astype(jnp.float32)
-    final = layer_norm(second, vector(3), vector(4))
-    for t in range(n_req):
-        for g in range(n_mdl):
-            send5[t, g] = final[
-                t * pos_dev : (t + 1) * pos_dev, g * width : (g + 1) * width
-            ].astype(jnp.bfloat16)
+        ff_ref[k] = mm(active, w2_v[...]).reshape(2, rows_k, full)
+
+    def feed_near(k):
+        near_n[k].wait()
+        feed(k, m // 2)
+        part3[k, 2] = ff_ref[k, core % 2].astype(jnp.bfloat16)
+        second[k] = second[k] + ff_ref[k, m % 2].astype(jnp.bfloat16).astype(jnp.float32)
+        return push(part3.at[k, 2], recv3.at[k, 2], ssem3, rsem3, 3 * k + 2, core)
+
+    def feed_far(k):
+        passed_n[k].wait()
+        feed(k, 1 - m // 2)
+        part3[k, 0] = ff_ref[k, diag % 2].astype(jnp.bfloat16)
+        return push(part3.at[k, 0], recv3.at[k, 0], ssem3, rsem3, 3 * k, core)
+
+    def cross(k, mid):
+        mid.wait()
+        total = ff_ref[k, across % 2] + recv3[k, 0].astype(jnp.float32)
+        part3[k, 1] = total.astype(jnp.bfloat16)
+        return push(part3.at[k, 1], recv3.at[k, 1], ssem3, rsem3, 3 * k + 1, across)
+
     me = r * n_mdl + m
-    copies5 = []
-    for n, (i, j) in enumerate(others):
-        to_r, to_m = (r + i) % n_req, (m + j) % n_mdl
-        copy = pltpu.make_async_remote_copy(
-            src_ref=send5.at[to_r, to_m],
-            dst_ref=recv5.at[me],
-            send_sem=ssem5.at[n],
-            recv_sem=rsem5.at[n],
-            device_id=(to_r, to_m),
-            device_id_type=MESH,
-        )
-        copy.start()
-        copies5.append(copy)
-    recv5[me] = send5[r, m]
-    for copy in copies5:
-        copy.wait()
+
+    def finish(k, near, far):
+        near.wait()
+        hidden = second[k] + recv3[k, 2].astype(jnp.float32)
+        far.wait()
+        hidden = hidden + recv3[k, 1].astype(jnp.float32)
+        final = layer_norm(hidden, vector(3), vector(4))
+        for t in range(half):
+            for g in range(n_mdl):
+                send5[2 * t + k, g] = final[
+                    t * pos_dev : (t + 1) * pos_dev, g * width : (g + 1) * width
+                ].astype(jnp.bfloat16)
+        for i in range(half):
+            for j in range(n_mdl):
+                to_r = (r // 2 + i) % half * 2 + k
+                to_m = (m + j) % n_mdl
+                copy = pltpu.make_async_remote_copy(
+                    src_ref=send5.at[to_r, to_m],
+                    dst_ref=recv5.at[me],
+                    send_sem=ssem5,
+                    recv_sem=rsem5,
+                    device_id=(to_r, to_m),
+                    device_id_type=MESH,
+                )
+                if i == 0 and j == 0:
+
+                    @pl.when(r % 2 == k)
+                    def _():
+                        recv5[me] = send5[r, m]
+
+                    @pl.when(r % 2 != k)
+                    def _():
+                        copy.start()
+
+                else:
+                    copy.start()
+
+    pass_on(0)
+    near_0 = feed_near(0)
+    pass_on(1)
+    mid_0 = feed_far(0)
+    near_1 = feed_near(1)
+    far_0 = cross(0, mid_0)
+    mid_1 = feed_far(1)
+    far_1 = cross(1, mid_1)
+    finish(0, near_0, far_0)
+    finish(1, near_1, far_1)
+    n_others = n_req * n_mdl - 1
+    pltpu.make_async_copy(recv5.at[:n_others], recv5.at[:n_others], ssem5).wait()
+    pltpu.make_async_copy(recv5.at[:n_others], recv5.at[:n_others], rsem5).wait()
     arrived = recv5[...].astype(jnp.float32).reshape(rows, width).astype(jnp.bfloat16)
     out_ref[...] = mm(home, arrived).astype(jnp.bfloat16)
 
@@ -630,37 +702,37 @@
             scratch_shapes=[pltpu.VMEM(a.shape, a.dtype) for a in large]
             + [
                 pltpu.VMEM((rows, rows), f32),
-                pltpu.VMEM((n_req, rows // n_req, width), bf16),
-                pltpu.VMEM((n_req, rows // n_req, width), bf16),
-                pltpu.VMEM((n_mdl, rows, width), bf16),
+                pltpu.VMEM((n_req, per_dev, pos_dev, width), bf16),
+                pltpu.VMEM((n_mdl, per_dev, n_req, pos_dev, width), bf16),
                 pltpu.VMEM((n_mdl, 8, width), f32),
                 pltpu.VMEM((3, rows, width), f32),
                 pltpu.VMEM((rows, width), bf16),
                 pltpu.VMEM((rows, width), bf16),
                 pltpu.VMEM((rows, width), bf16),
                 pltpu.VMEM((per_dev, draft, draft), f32),
-                pltpu.VMEM((n_mdl, draft, full), bf16),
-                pltpu.VMEM((n_mdl, draft, full), bf16),
-                pltpu.VMEM((n_mdl, draft, full), bf16),
-                pltpu.VMEM((n_mdl, draft, full), bf16),
-                pltpu.VMEM((n_mdl, draft, full), bf16),
+                pltpu.VMEM((3, draft, full), bf16),
+                pltpu.VMEM((3, draft, full), bf16),
+                pltpu.VMEM((2, n_mdl, draft // 2, full), bf16),
+                pltpu.VMEM((2, 2, draft // 2, full), f32),
+                pltpu.VMEM((2, 3, draft // 2, full), bf16),
+                pltpu.VMEM((2, 3, draft // 2, full), bf16),
                 pltpu.VMEM((n_req, n_mdl, pos_dev, width), bf16),
                 pltpu.VMEM((n_all, pos_dev, width), bf16),
                 dma((9,)),
                 dma((n_req,)),
                 dma((n_req,)),
+                dma((n_req + 2,)),
+                dma((n_req + 2,)),
                 dma((3,)),
                 dma((3,)),
                 dma((3,)),
                 dma((3,)),
-                dma((3,)),
-                dma((3,)),
-                dma((3,)),
-                dma((3,)),
-                dma((3,)),
-                dma((3,)),
-                dma((n_all,)),
-                dma((n_all,)),
+                dma((6,)),
+                dma((6,)),
+                dma((6,)),
+                dma((6,)),
+                dma,
+                dma,
             ],
             compiler_params=pltpu.CompilerParams(
                 collective_id=0, has_side_effects=True, vmem_limit_bytes=56 * 2**20
@@ -696,7 +768,8 @@
     per_dev, draft = args[19].shape
     n_mdl = lax.axis_size("mdl")
     whole_positions = rows % requests == 0 and rows // requests == 8
-    if whole_positions and per_dev == n_mdl == 4 and per_dev * draft == rows:
+    fits = lax.axis_size("req") == 8 and draft == 64
+    if fits and whole_positions and per_dev == n_mdl == 4 and per_dev * draft == rows:
         return per_device_fused(*args)
     return per_device_general(*args)
 

time: 52.7 us -> 45.2 us (0.86)
  Pallas kernels: 47.6 us -> 40.2 us
    pallas_call x1, Pallas kernels: 47.6 us -> 40.2 us  [per_device_fused(): pl.pallas_call(functools.partial(fused_kernel, key_pool.shape[0]), out_sh...]
where the time goes in v2:
time: 45.2 us; the launch traced here: 45 us
  Pallas kernels  40.2 us (89%)
  local copies, waits for them, and re-layouts  4.12 us (9%)
  between operations  0.66 us (1%)
    pallas_call x1, Pallas kernels, per_device_fused(): pl.pallas_call(functools.partial(fused_kernel, key_pool.shape[0]), out_sh...  40.2 us
    unnamed x9, local copies, waits for them, and re-layouts  3.55 us

profile of v2, /device:TPU:0, one launch (start us, length us, event | category | flops | bytes accessed | tf_op | source)
XLA Modules:
  0.0 45.0 jit_solution(3133086685321840799)
XLA Ops:
  0.6 0.0 copy-start.2
  0.6 0.6 %copy-done.2 = bf16[256]{0:T(256)(128)(2,1)S(1)} copy-done((bf16[256]{0:T(256)(128)(2,1)S(1)}, bf16[256]{0:T(256)(128)(2,1)}, u32[]{:S(2)}) %copy-start.2) | copy-done | bytes 536
  1.3 0.6 %broadcast_in_dim.21.q_bias_ref = bf16[1,256]{1,0:T(2,128)(2,1)} reshape(bf16[256]{0:T(256)(128)(2,1)S(1)} %copy-done.2) | data formatting | bytes 1024 | tf_op jit(solution)/shard_map/broadcast_in_dim | solution.py:746
  1.9 40.2 %shard_map.220 = (bf16[256,256]{1,0:T(8,128)(2,1)}, bf16[4,8,256]{2,1,0:T(8,128)(2,1)}, bf16[4,8,256]{2,1,0:T(8,128)(2,1)}) custom-call(s32[32]{0:T(128)} %perm_ref.1, s32[4,4]{1,0:T(4,128)} %page_ref.1, s32[4]{0:T(128)} %len_ref.1, s32[4,8]{1,0:T(4,128)} %accepted_ref.1, s32[4,64]{1,0:T(4,128)} %parents_ref.1, bf16[1,256]{1,0:T(2,128)(2,1)} %broadcast_in_dim.21.q_bias_ref, ...), custom_call_target="tpu_custom_call" | custom-call | tf_op jit(solution)/shard_map/pallas_call | solution.py:697
  42.1 0.0 copy-start.1
  42.1 1.6 %copy.27 = bf16[256,256]{1,0:T(8,128)(2,1)} copy(bf16[256,256]{1,0:T(8,128)(2,1)} %get-tuple-element.6) | data formatting | bytes 262144
  43.6 0.0 copy-done.1
  43.7 0.0 copy-start
  43.7 0.6 %copy.28 = bf16[4,8,256]{2,1,0:T(8,128)(2,1)} copy(bf16[4,8,256]{2,1,0:T(8,128)(2,1)S(1)} %copy-done.1) | data formatting | bytes 32768
  44.3 0.1 copy-done
  44.4 0.6 %copy.29 = bf16[4,8,256]{2,1,0:T(8,128)(2,1)} copy(bf16[4,8,256]{2,1,0:T(8,128)(2,1)S(1)} %copy-done) | data formatting | bytes 32768
Async XLA Ops:
  0.6 0.7 %copy-start.2 = (bf16[256]{0:T(256)(128)(2,1)S(1)}, bf16[256]{0:T(256)(128)(2,1)}, u32[]{:S(2)}) copy-start(bf16[256]{0:T(256)(128)(2,1)} %param.24) | copy-start | bytes 1540
  42.1 1.6 %copy-start.1 = (bf16[4,8,256]{2,1,0:T(8,128)(2,1)S(1)}, bf16[4,8,256]{2,1,0:T(8,128)(2,1)}, u32[]{:S(2)}) copy-start(bf16[4,8,256]{2,1,0:T(8,128)(2,1)} %get-tuple-element.7) | copy-start | bytes 49156
  43.7 0.7 %copy-start = (bf16[4,8,256]{2,1,0:T(8,128)(2,1)S(1)}, bf16[4,8,256]{2,1,0:T(8,128)(2,1)}, u32[]{:S(2)}) copy-start(bf16[4,8,256]{2,1,0:T(8,128)(2,1)} %get-tuple-element.8) | copy-start | bytes 49156
